TPU v7x, 256 devices: a whole 4x4x8 slice. The times are simulated.
256 devices in a mesh: gx: 8 (over y, core), gy: 32 (over x, z).
Axes of the slice: x: 4, y: 4, z: 8, core: 2. Of those that a mesh axis runs over, the one named last changes fastest.
Arguments:
- flow_field: float32 [16, 256, 256, 128], P(None, 'gx', 'gy'), may hold values from -6 to 6
- cotangent: float32 [16, 256, 256, 128], P(None, 'gx', 'gy'), may hold values from -6 to 6
- mode_weights: float32 [4, 16, 16, 256], replicated, may hold values from -3 to 3
- point_weights: float32 [16, 16], replicated, may hold values from -1.5 to 1.5
- point_bias: float32 [16], replicated, may hold values from -3 to 3
Outputs:
- output_field: float32 [16, 256, 256, 128], P(None, 'gx', 'gy')
- grad_field: float32 [16, 256, 256, 128], P(None, 'gx', 'gy')
- grad_modes: float32 [4, 16, 16, 256], replicated
- grad_point: float32 [16, 16], replicated
- grad_bias: float32 [16], replicated
All inputs are finite; a program needn't handle non-finite values.
Results may differ from a plain program's by a relative error of at most 0.00024.
Values sent between devices are 32-bit elements; how exact they have to be, the bound alone decides.
No kernel may reach another device: no remote copies, remote signals or barrier semaphores. Data moves between devices by JAX's collectives and lax.ppermute only.
A program may use at most 128 MiB of HBM per device.

v0:
```python
import math
import jax
import jax.numpy as jnp
from jax import lax
from jax.sharding import PartitionSpec as P

LOW_PASS = [
    0.23037781330885523,
    0.7148465705525415,
    0.6308807679295904,
    -0.02798376941698385,
    -0.18703481171888114,
    0.030841381835986965,
    0.032883011666982945,
    -0.010597401784997278,
]
HIGH_PASS = [(-1) ** position * LOW_PASS[7 - position] for position in range(8)]
GELU_SCALE = 0.7978845608028654
GELU_CUBE = 0.044715


def from_behind(value, axis, by):
    devices = lax.axis_size(axis)
    return lax.ppermute(value, axis, [(i, (i + by) % devices) for i in range(devices)])


def filter_table(filter_taps, out_count, in_count, periodic):
    row_index = lax.broadcasted_iota(jnp.int32, (out_count, in_count), 0)
    col_index = lax.broadcasted_iota(jnp.int32, (out_count, in_count), 1)
    offset = col_index - 2 * row_index
    if periodic:
        offset = offset % in_count
    matrix = jnp.zeros((out_count, in_count), jnp.float32)
    for position in range(8):
        matrix = matrix + filter_taps[position] * (offset == position).astype(jnp.float32)
    return matrix


def lifted_table(filter_taps, out_count, in_count):
    row_index = lax.broadcasted_iota(jnp.int32, (out_count, in_count), 0)
    col_index = lax.broadcasted_iota(jnp.int32, (out_count, in_count), 1)
    offset = row_index - 2 * col_index + 6
    matrix = jnp.zeros((out_count, in_count), jnp.float32)
    for position in range(8):
        matrix = matrix + filter_taps[position] * (offset == position).astype(jnp.float32)
    return matrix


def along_x(matrix, signal):
    return jnp.einsum("kr,arys->akys", matrix, signal, precision=lax.Precision.HIGHEST)


def along_y(matrix, signal):
    return jnp.einsum("kr,axrs->axks", matrix, signal, precision=lax.Precision.HIGHEST)


def plane_x(matrix, signal):
    return jnp.einsum("kr,ary->aky", matrix, signal, precision=lax.Precision.HIGHEST)


def plane_y(matrix, signal):
    return jnp.einsum("kr,axr->axk", matrix, signal, precision=lax.Precision.HIGHEST)


def to_lanes(signal):
    channels, extent_x, extent_y, planes = signal.shape
    return jnp.transpose(signal, (0, 3, 1, 2)).reshape(channels * planes, extent_x, extent_y)


def from_lanes(signal, channels):
    stacked, extent_x, extent_y = signal.shape
    return jnp.transpose(
        signal.reshape(channels, stacked // channels, extent_x, extent_y), (0, 2, 3, 1)
    )


def four_bands(signal):
    extent_x, extent_y = (signal.shape[1], signal.shape[2])
    low_x = plane_x(filter_table(LOW_PASS, extent_x // 2, extent_x, True), signal)
    high_x = plane_x(filter_table(HIGH_PASS, extent_x // 2, extent_x, True), signal)
    low_y = filter_table(LOW_PASS, extent_y // 2, extent_y, True)
    high_y = filter_table(HIGH_PASS, extent_y // 2, extent_y, True)
    return jnp.stack(
        [
            plane_y(low_y, low_x),
            plane_y(low_y, high_x),
            plane_y(high_y, low_x),
            plane_y(high_y, high_x),
        ]
    )


def join_bands(changes):
    modes_x, modes_y = (changes.shape[2], changes.shape[3])
    low_x = filter_table(LOW_PASS, modes_x, 2 * modes_x, True).T
    high_x = filter_table(HIGH_PASS, modes_x, 2 * modes_x, True).T
    low_y = filter_table(LOW_PASS, modes_y, 2 * modes_y, True).T
    high_y = filter_table(HIGH_PASS, modes_y, 2 * modes_y, True).T
    from_low = plane_y(low_y, changes[0]) + plane_y(high_y, changes[2])
    from_high = plane_y(low_y, changes[1]) + plane_y(high_y, changes[3])
    return plane_x(low_x, from_low) + plane_x(high_x, from_high)


def gelu_parts(signal):
    tangent = jnp.tanh(GELU_SCALE * (signal + GELU_CUBE * signal * signal * signal))
    activated = 0.5 * signal * (1.0 + tangent)
    gelu_slope = 0.5 * (1.0 + tangent) + 0.5 * signal * (1.0 - tangent * tangent) * GELU_SCALE * (
        1.0 + 3.0 * GELU_CUBE * signal * signal
    )
    return (activated, gelu_slope)


def wave_block(signal, weights_grid, transposed):
    x_index = lax.axis_index("gx")
    channels = signal.shape[0]
    extent_x, extent_y = (signal.shape[1], signal.shape[2])
    margin = from_behind(signal[:, :6], "gx", -1)
    halved = along_x(
        filter_table(LOW_PASS, extent_x // 2, extent_x + 6, False),
        jnp.concatenate([signal, margin], 1),
    )
    margin = from_behind(halved[:, :, :6], "gy", -1)
    level_one = along_y(
        filter_table(LOW_PASS, extent_y // 2, extent_y + 6, False),
        jnp.concatenate([halved, margin], 2),
    )
    level_one = to_lanes(lax.all_to_all(level_one, "gy", split_axis=3, concat_axis=2, tiled=True))
    rows_one, cols_one = (level_one.shape[1], level_one.shape[2])
    margin = from_behind(level_one[:, :6], "gx", -1)
    level_two = plane_x(
        filter_table(LOW_PASS, rows_one // 2, rows_one + 6, False),
        jnp.concatenate([level_one, margin], 1),
    )
    level_two = plane_y(filter_table(LOW_PASS, cols_one // 2, cols_one, True), level_two)
    rows_two, cols_two = (level_two.shape[1], level_two.shape[2])
    margin = from_behind(level_two[:, :6], "gx", -1)
    level_three = plane_x(
        filter_table(LOW_PASS, rows_two // 2, rows_two + 6, False),
        jnp.concatenate([level_two, margin], 1),
    )
    level_three = plane_y(filter_table(LOW_PASS, cols_two // 2, cols_two, True), level_three)
    gathered = lax.all_gather(level_three, "gx", axis=1, tiled=True)
    wave_bands = four_bands(gathered)
    stacked, modes_x, modes_y = (wave_bands.shape[1], wave_bands.shape[2], wave_bands.shape[3])
    split_bands = wave_bands.reshape(4, channels, stacked // channels, modes_x, modes_y)
    if transposed:
        mixed_bands = jnp.einsum(
            "bozxy,bioxy->bizxy", split_bands, weights_grid, precision=lax.Precision.HIGHEST
        )
    else:
        mixed_bands = jnp.einsum(
            "bizxy,bioxy->bozxy", split_bands, weights_grid, precision=lax.Precision.HIGHEST
        )
    delta_three = join_bands((mixed_bands - split_bands).reshape(4, stacked, modes_x, modes_y))
    own_rows = rows_two // 2
    own_part = lax.dynamic_slice_in_dim(delta_three, x_index * own_rows, own_rows, 1)
    margin = from_behind(own_part[:, own_rows - 3 :], "gx", 1)
    delta_two = plane_x(
        lifted_table(LOW_PASS, 2 * own_rows, own_rows + 3), jnp.concatenate([margin, own_part], 1)
    )
    cols_three = own_part.shape[2]
    delta_two = plane_y(filter_table(LOW_PASS, cols_three, 2 * cols_three, True).T, delta_two)
    margin = from_behind(delta_two[:, rows_two - 3 :], "gx", 1)
    delta_one = plane_x(
        lifted_table(LOW_PASS, 2 * rows_two, rows_two + 3), jnp.concatenate([margin, delta_two], 1)
    )
    delta_one = plane_y(filter_table(LOW_PASS, cols_two, 2 * cols_two, True).T, delta_one)
    returned = lax.all_to_all(
        from_lanes(delta_one, channels), "gy", split_axis=2, concat_axis=3, tiled=True
    )
    rows_back = returned.shape[1]
    margin = from_behind(returned[:, rows_back - 3 :], "gx", 1)
    widened = along_x(
        lifted_table(LOW_PASS, 2 * rows_back, rows_back + 3), jnp.concatenate([margin, returned], 1)
    )
    cols_back = widened.shape[2]
    margin = from_behind(widened[:, :, cols_back - 3 :], "gy", 1)
    delta_zero = along_y(
        lifted_table(LOW_PASS, 2 * cols_back, cols_back + 3), jnp.concatenate([margin, widened], 2)
    )
    return (signal + delta_zero, split_bands)


def local(flow_field, cotangent, mode_weights, point_weights, point_bias):
    channels = flow_field.shape[0]
    modes_x = flow_field.shape[1] * lax.axis_size("gx") // 16
    modes_y = flow_field.shape[2] * lax.axis_size("gy") // 16
    weights_grid = mode_weights.reshape(4, channels, channels, modes_x, modes_y)
    spectral_flow, bands_flow = wave_block(flow_field, weights_grid, False)
    pointwise = jnp.einsum(
        "io,ixys->oxys", point_weights, flow_field, precision=lax.Precision.HIGHEST
    )
    before_gelu = spectral_flow + pointwise + point_bias[:, None, None, None]
    output_field, gelu_slope = gelu_parts(before_gelu)
    grad_inner = cotangent * gelu_slope
    spectral_grad, bands_grad = wave_block(grad_inner, weights_grid, True)
    point_back = jnp.einsum(
        "io,oxys->ixys", point_weights, grad_inner, precision=lax.Precision.HIGHEST
    )
    grad_field = spectral_grad + point_back
    mode_local = jnp.einsum(
        "bizxy,bozxy->bioxy", bands_flow, bands_grad, precision=lax.Precision.HIGHEST
    )
    mode_local = mode_local.reshape(4, channels, channels, modes_x * modes_y)
    mode_total = lax.psum(mode_local, "gy")
    point_local = jnp.einsum(
        "ixys,oxys->io", flow_field, grad_inner, precision=lax.Precision.HIGHEST
    )
    bias_local = jnp.sum(grad_inner, axis=(1, 2, 3))
    point_total, bias_total = lax.psum((point_local, bias_local), ("gx", "gy"))
    plane_total = flow_field.shape[3]
    cell_count = (
        plane_total
        * flow_field.shape[1]
        * flow_field.shape[2]
        * lax.axis_size("gx")
        * lax.axis_size("gy")
    )
    grad_modes = mode_total / math.sqrt(plane_total)
    grad_point = point_total / math.sqrt(cell_count)
    grad_bias = bias_total / math.sqrt(cell_count)
    return (output_field, grad_field, grad_modes, grad_point, grad_bias)


def solution(mesh):
    in_specs = (P(None, "gx", "gy", None), P(None, "gx", "gy", None), P(), P(), P())
    out_specs = (P(None, "gx", "gy", None), P(None, "gx", "gy", None), P(), P(), P())
    return jax.shard_map(local, mesh=mesh, in_specs=in_specs, out_specs=out_specs, check_vma=False)
```

profile of v0, /device:TPU:8, one launch (start us, length us, event | category | flops | bytes accessed | tf_op | source)
XLA Modules:
  0.0 609.2 jit_solution(3356555167298708479)
XLA Ops:
  9.3 6.7 %collective-permute-done = f32[16,6,8,128]{3,1,2,0:T(8,128)S(1)} collective-permute-done((f32[16,6,8,128]{3,1,2,0:T(8,128)S(1)}, f32[16,6,8,128]{3,1,2,0:T(8,128)S(1)}, u32[]{:S(2)}, u32[]{:S(2)}) %collective-permute-start) | collective-permute-done | bytes 393248 | tf_op jit(solution)/shard_map/ppermute | solution.py:24
  17.9 8.1 %collective-permute-start.1 = (f32[16,16,6,128]{3,1,2,0:T(8,128)S(1)}, f32[16,16,6,128]{3,1,2,0:T(8,128)S(1)}, u32[]{:S(2)}, u32[]{:S(2)}) collective-permute-start(f32[16,16,6,128]{3,1,2,0:T(8,128)S(1)} %slice.105), channel_id=1, source_target_pairs={{0,31},{1,0},{2,1},{3,2},{4,3},{5,4},{6,5},{7,6},{8,7},{9,8},{10,9... | collective-permute-start | bytes 2359304 | tf_op jit(solution)/shard_map/ppermute | solution.py:24
  26.0 17.1 %collective-permute-done.1 = f32[16,16,6,128]{3,1,2,0:T(8,128)S(1)} collective-permute-done((f32[16,16,6,128]{3,1,2,0:T(8,128)S(1)}, f32[16,16,6,128]{3,1,2,0:T(8,128)S(1)}, u32[]{:S(2)}, u32[]{:S(2)}) %collective-permute-start.1) | collective-permute-done | bytes 786464 | tf_op jit(solution)/shard_map/ppermute | solution.py:24
  54.1 7.6 %all-to-all-start = ((f32[32,1,4096]{2,1,0:T(1,128)}), f32[32,1,4096]{2,1,0:T(1,128)S(1)}, u32[]{:S(2)}, u32[]{:S(2)}) async-start(f32[32,1,4096]{2,1,0:T(1,128)} %reshape.86), calls=%async_computation | async-start | bytes 1048576 | tf_op jit(solution)/shard_map/all_to_all | solution.py:127
  61.7 6.2 %copy.304 = f32[4,16,16,256]{2,1,3,0:T(8,128)} copy(f32[4,16,16,256]{3,2,1,0:T(8,128)S(1)} %copy-done.4) | data formatting | bytes 2097152 | tf_op jit(solution)/shard_map/reshape | solution.py:188
  68.0 11.4 %all-to-all-done = f32[32,1,4096]{2,1,0:T(1,128)S(1)} async-done(((f32[32,1,4096]{2,1,0:T(1,128)}), f32[32,1,4096]{2,1,0:T(1,128)S(1)}, u32[]{:S(2)}, u32[]{:S(2)}) %all-to-all-start) | async-done | bytes 524320 | tf_op jit(solution)/shard_map/all_to_all | solution.py:127
  84.6 4.8 copy.211
  105.0 14.3 %all_gather.6 = f32[64,32,32]{0,2,1:T(8,128)S(1)} all-gather(f32[64,4,32]{0,2,1:T(8,128)S(1)} %fusion.123), channel_id=1, replica_groups=mesh['gx'=8,'gy'=32] {'gx'}, dimensions={1}, use_global_device_ids=true | all-gather | bytes 294912 | tf_op jit(solution)/shard_map/all_gather | solution.py:142
  125.7 14.9 %bitcast_subtract_fusion.1 = f32[4,16,4,16,16]{1,2,4,3,0:T(4,128)S(1)} fusion(f32[4,16,16,16,16]{2,1,4,3,0:T(8,128)} %bitcast.264, f32[1,16,4,16,16]{1,2,4,3,0:T(4,128)S(1)} %copy.227, f32[1,16,4,16,16]{1,2,4,3,0:T(4,128)S(1)} %copy.226, f32[1,16,4,16,16]{1,2,4,3,0:T(4,128)S(1)} %copy.225, f32[1,16,4,16,16]{1,2,4,3,0:T(4,128)S(1)} %copy.224), kind=kOutput, calls=%fused_computation.23 | convolution fusion | flops 13041664 | bytes 1572864 | tf_op jit(solution)/shard_map/bizxy,bioxy->bozxy/dot_general | solution.py:151
  150.9 4.8 collective-permute-done.4
  166.7 4.8 bitcast_bitcast_fusion.1
  175.0 22.0 %all_to_all.72 = f32[32,1,4096]{2,1,0:T(1,128)S(1)} all-to-all(f32[32,1,4096]{2,1,0:T(1,128)S(1)} %reshape.88), channel_id=1, replica_groups=mesh['gx'=8,'gy'=32] {'gy'}, dimensions={0} | all-to-all | bytes 1048576 | tf_op jit(solution)/shard_map/all_to_all | solution.py:168
  201.8 4.7 copy.242
  220.1 15.0 %collective-permute-done.7 = f32[16,32,3,128]{3,1,2,0:T(8,128)S(1)} collective-permute-done((f32[16,32,3,128]{3,1,2,0:T(8,128)S(1)}, f32[16,32,3,128]{3,1,2,0:T(8,128)S(1)}, u32[]{:S(2)}, u32[]{:S(2)}) %collective-permute-start.7) | collective-permute-done | bytes 786464 | tf_op jit(solution)/shard_map/ppermute | solution.py:24
  235.3 6.6 %fusion.1133 = (f32[16]{0:T(128)}, f32[16,32,8,128]{3,2,1,0:T(8,128)S(1)}, f32[16,32,8,128]{3,2,1,0:T(8,128)}) fusion(f32[16,32,8,128]{3,2,1,0:T(8,128)S(1)} %copy-done.20, f32[16]{0:T(128)S(1)} %copy-done.21, f32[16,32,8,128]{3,0,2,1:T(8,128)S(1)} %fusion.27, f32[16,32,8,128]{3,2,1,0:T(8,128)S(1)} %copy-done.1, s32[7]{0:T(128)S(1)} %iota_multiply_fusion.2, ...), kind=kOutput, calls=%fused_computation.1198 | convolution fusion | flops 56100200 | bytes 12320924 | tf_op jit(solution)/shard_map/kr,axrs->axks/dot_general | solution.py:54
  241.9 5.3 collective-permute-done.8
  249.6 19.6 %collective-permute-done.9 = f32[16,16,6,128]{3,1,2,0:T(8,128)S(1)} collective-permute-done((f32[16,16,6,128]{3,1,2,0:T(8,128)S(1)}, f32[16,16,6,128]{3,1,2,0:T(8,128)S(1)}, u32[]{:S(2)}, u32[]{:S(2)}) %collective-permute-start.9) | collective-permute-done | bytes 786464 | tf_op jit(solution)/shard_map/ppermute | solution.py:24
  279.4 19.5 %all_to_all.73 = f32[32,1,4096]{2,1,0:T(1,128)S(1)} all-to-all(f32[32,1,4096]{2,1,0:T(1,128)S(1)} %reshape.90), channel_id=1, replica_groups=mesh['gx'=8,'gy'=32] {'gy'}, dimensions={0} | all-to-all | bytes 1048576 | tf_op jit(solution)/shard_map/all_to_all | solution.py:127
  303.6 4.8 copy.253
  319.1 5.1 collective-permute-done.11
  325.1 17.3 %all_gather.7 = f32[64,32,32]{0,2,1:T(8,128)S(1)} all-gather(f32[64,4,32]{0,2,1:T(8,128)S(1)} %fusion.119), channel_id=1, replica_groups=mesh['gx'=8,'gy'=32] {'gx'}, dimensions={1}, use_global_device_ids=true | all-gather | bytes 294912 | tf_op jit(solution)/shard_map/all_gather | solution.py:142
  350.4 18.2 %bitcast_subtract_fusion = f32[4,16,4,16,16]{1,2,4,3,0:T(4,128)S(1)} fusion(f32[4,16,16,16,16]{2,1,4,3,0:T(8,128)} %bitcast.265, f32[1,16,4,16,16]{1,2,4,3,0:T(4,128)} %copy.269, f32[1,16,4,16,16]{1,2,4,3,0:T(4,128)} %copy.268, f32[1,16,4,16,16]{1,2,4,3,0:T(4,128)} %copy.267, f32[1,16,4,16,16]{1,2,4,3,0:T(4,128)S(1)} %copy.266), kind=kOutput, calls=%fused_computation.19 | convolution fusion | flops 13041664 | bytes 1572864 | tf_op jit(solution)/shard_map/bozxy,bioxy->bizxy/dot_general | solution.py:147
  384.9 4.8 collective-permute-done.12
  400.7 4.7 bitcast_bitcast_fusion
  409.7 5.7 all-to-all-start.3
  415.5 17.6 %fusion.86 = f32[4,16,16,16,16]{4,3,2,1,0:T(8,128)} fusion(f32[1,16,4,16,16]{1,2,4,3,0:T(4,128)} %copy.269, f32[1,16,4,16,16]{1,2,4,3,0:T(4,128)} %copy.268, f32[1,16,4,16,16]{1,2,4,3,0:T(4,128)} %copy.267, f32[1,16,4,16,16]{1,2,4,3,0:T(4,128)} %copy-done.10, f32[1,16,4,16,16]{1,2,4,3,0:T(4,128)} %copy-done.9, f32[1,16,4,16,16]{1,2,4,3,0:T(4,128)} %copy-done.7, ...), kind=kOutput, calls=%fused_computation.106 | convolution fusion | flops 12976128 | bytes 1572864 | tf_op jit(solution)/shard_map/bizxy,bozxy->bioxy/dot_general | solution.py:201
  433.0 7.7 %copy.290 = f32[4,16,16,256]{3,2,1,0:T(8,128)} copy(f32[4,16,16,256]{1,2,3,0:T(8,128)} %bitcast.266) | data formatting | bytes 2097152 | tf_op jit(solution)/shard_map/reshape | solution.py:204
  440.8 6.3 %fusion.45 = f32[16,16]{0,1:T(8,128)S(1)} fusion(f32[16,32,8,128]{3,2,1,0:T(8,128)} %param.5, f32[16,32,8,128]{3,2,1,0:T(8,128)S(1)} %get-tuple-element.28), kind=kOutput, calls=%fused_computation.66 | convolution fusion | flops 100663296 | bytes 4195328 | tf_op jit(solution)/shard_map/ixys,oxys->io/dot_general | solution.py:206
  447.1 77.5 %all-reduce = (f32[16,16]{0,1:T(8,128)S(1)}, f32[16]{0:T(128)S(1)}) all-reduce(f32[16,16]{0,1:T(8,128)S(1)} %fusion.45, f32[16]{0:T(128)S(1)} %copy-done.19), channel_id=1, replica_groups=mesh['gx'=8,'gy'=32] {'gx','gy'}, use_global_device_ids=true, to_apply=%region_1.2 | all-reduce | flops 272 | bytes 2176 | tf_op jit(solution)/shard_map/psum | solution.py:210
  529.3 4.8 copy.284
  551.4 41.4 %all-reduce.3.cloned.1.call-done = f32[4,16,16,256]{3,2,1,0:T(8,128)} async-done(((f32[4,16,16,256]{3,2,1,0:T(8,128)}), f32[4,16,16,256]{3,2,1,0:T(8,128)}) %all-reduce.3.cloned.1.call-update) | async-done | bytes 1048592 | tf_op jit(solution)/shard_map/psum | solution.py:205
  596.9 5.2 bitcast_add_fusion
  (201 shorter events, 179.4 us)
Async XLA Ops:
  7.2 210.0 %copy-start = (f32[16,16]{1,0:T(8,128)S(1)}, f32[16,16]{1,0:T(8,128)}, u32[]{:S(2)}) copy-start(f32[16,16]{1,0:T(8,128)} %param.8) | copy-start | bytes 3076
  9.2 6.7 %collective-permute-start = (f32[16,6,8,128]{3,1,2,0:T(8,128)S(1)}, f32[16,6,8,128]{3,1,2,0:T(8,128)S(1)}, u32[]{:S(2)}, u32[]{:S(2)}) collective-permute-start(f32[16,6,8,128]{3,1,2,0:T(8,128)S(1)} %slice.104), channel_id=1, source_target_pairs={{0,224},{32,0},{64,32},{96,64},{128,96},{160,128},{192,160},{224,1... | collective-permute-start | bytes 1179656 | tf_op jit(solution)/shard_map/ppermute | solution.py:24
  17.9 25.2 %collective-permute-start.1 = (f32[16,16,6,128]{3,1,2,0:T(8,128)S(1)}, f32[16,16,6,128]{3,1,2,0:T(8,128)S(1)}, u32[]{:S(2)}, u32[]{:S(2)}) collective-permute-start(f32[16,16,6,128]{3,1,2,0:T(8,128)S(1)} %slice.105), channel_id=1, source_target_pairs={{0,31},{1,0},{2,1},{3,2},{4,3},{5,4},{6,5},{7,6},{8,7},{9,8},{10,9... | collective-permute-start | bytes 2359304 | tf_op jit(solution)/shard_map/ppermute | solution.py:24
  49.8 12.0 %copy-start.4 = (f32[4,16,16,256]{3,2,1,0:T(8,128)S(1)}, f32[4,16,16,256]{3,2,1,0:T(8,128)}, u32[]{:S(2)}) copy-start(f32[4,16,16,256]{3,2,1,0:T(8,128)} %param.7) | copy-start | bytes 3145732
  54.1 25.3 %all-to-all-start = ((f32[32,1,4096]{2,1,0:T(1,128)}), f32[32,1,4096]{2,1,0:T(1,128)S(1)}, u32[]{:S(2)}, u32[]{:S(2)}) async-start(f32[32,1,4096]{2,1,0:T(1,128)} %reshape.86), calls=%async_computation | async-start | bytes 1048576 | tf_op jit(solution)/shard_map/all_to_all | solution.py:127
  93.2 3.9 collective-permute-start.2
  98.2 5.8 collective-permute-start.3
  100.1 224.6 %copy-start.15 = (s32[32]{0:T(128)}, s32[32]{0:T(128)S(1)}, u32[]{:S(2)}) copy-start(s32[32]{0:T(128)S(1)} %iota_multiply_fusion.3) | copy-start | bytes 388
  150.8 5.0 collective-permute-start.4
  150.9 84.3 %copy-start.11 = (s32[7]{0:T(128)}, s32[7]{0:T(128)S(1)}, u32[]{:S(2)}) copy-start(s32[7]{0:T(128)S(1)} %iota_multiply_fusion.2) | copy-start | bytes 88
  156.7 4.1 collective-permute-start.5
  156.7 10.0 %copy-start.17 = (s32[11]{0:T(128)}, s32[11]{0:T(128)S(1)}, u32[]{:S(2)}) copy-start(s32[11]{0:T(128)S(1)} %iota_multiply_fusion.1) | copy-start | bytes 136
  209.3 7.9 %copy-start.1 = (f32[16,32,8,128]{3,2,1,0:T(8,128)S(1)}, f32[16,32,8,128]{3,2,1,0:T(8,128)}, u32[]{:S(2)}) copy-start(f32[16,32,8,128]{3,2,1,0:T(8,128)} %param.5) | copy-start | bytes 6291460
  209.3 4.4 collective-permute-start.6
  209.4 10.7 %copy-start.13 = (s32[19]{0:T(128)}, s32[19]{0:T(128)S(1)}, u32[]{:S(2)}) copy-start(s32[19]{0:T(128)S(1)} %iota_multiply_fusion) | copy-start | bytes 232
  214.9 20.2 %collective-permute-start.7 = (f32[16,32,3,128]{3,1,2,0:T(8,128)S(1)}, f32[16,32,3,128]{3,1,2,0:T(8,128)S(1)}, u32[]{:S(2)}, u32[]{:S(2)}) collective-permute-start(f32[16,32,3,128]{3,1,2,0:T(8,128)S(1)} %slice.115), channel_id=1, source_target_pairs={{0,1},{1,2},{2,3},{3,4},{4,5},{5,6},{6,7},{7,8},{8,9},{9,10},{10,1... | collective-permute-start | bytes 2359304 | tf_op jit(solution)/shard_map/ppermute | solution.py:24
  220.0 15.2 %copy-start.20 = (f32[16,32,8,128]{3,2,1,0:T(8,128)S(1)}, f32[16,32,8,128]{3,2,1,0:T(8,128)}, u32[]{:S(2)}) copy-start(f32[16,32,8,128]{3,2,1,0:T(8,128)} %param.6) | copy-start | bytes 6291460
  220.0 15.2 %copy-start.21 = (f32[16]{0:T(128)S(1)}, f32[16]{0:T(128)}, u32[]{:S(2)}) copy-start(f32[16]{0:T(128)} %param.9) | copy-start | bytes 196
  241.9 5.3 collective-permute-start.8
  249.5 19.7 %collective-permute-start.9 = (f32[16,16,6,128]{3,1,2,0:T(8,128)S(1)}, f32[16,16,6,128]{3,1,2,0:T(8,128)S(1)}, u32[]{:S(2)}, u32[]{:S(2)}) collective-permute-start(f32[16,16,6,128]{3,1,2,0:T(8,128)S(1)} %slice.117), channel_id=1, source_target_pairs={{0,31},{1,0},{2,1},{3,2},{4,3},{5,4},{6,5},{7,6},{8,7},{9,8},{10,9... | collective-permute-start | bytes 2359304 | tf_op jit(solution)/shard_map/ppermute | solution.py:24
  312.2 3.9 collective-permute-start.10
  317.2 7.0 %collective-permute-start.11 = (f32[64,6,64]{2,1,0:T(8,128)S(1)}, f32[64,6,64]{2,1,0:T(8,128)S(1)}, u32[]{:S(2)}, u32[]{:S(2)}) collective-permute-start(f32[64,6,64]{2,1,0:T(8,128)S(1)} %bitcast.290), channel_id=1, source_target_pairs={{0,224},{32,0},{64,32},{96,64},{128,96},{160,128},{192,160},{224,1... | collective-permute-start | bytes 294920 | tf_op jit(solution)/shard_map/ppermute | solution.py:24
  379.3 10.5 %copy-start.12 = (s32[7]{0:T(128)S(1)}, s32[7]{0:T(128)}, u32[]{:S(2)}) copy-start(s32[7]{0:T(128)} %copy-done.11) | copy-start | bytes 88
  379.3 10.8 %copy-start.16 = (s32[32]{0:T(128)S(1)}, s32[32]{0:T(128)}, u32[]{:S(2)}) copy-start(s32[32]{0:T(128)} %copy-done.15) | copy-start | bytes 388
  381.4 13.4 %copy-start.18 = (s32[11]{0:T(128)S(1)}, s32[11]{0:T(128)}, u32[]{:S(2)}) copy-start(s32[11]{0:T(128)} %copy-done.17) | copy-start | bytes 136
  384.8 5.0 collective-permute-start.12
  390.7 4.1 collective-permute-start.13
  405.5 10.0 %copy-start.6 = (f32[1,16,4,16,16]{1,2,4,3,0:T(4,128)S(1)}, f32[1,16,4,16,16]{1,2,4,3,0:T(4,128)}, u32[]{:S(2)}) copy-start(f32[1,16,4,16,16]{1,2,4,3,0:T(4,128)} %copy-done.5) | copy-start | bytes 196612
  409.7 114.9 %all-to-all-start.3 = ((f32[32,1,4096]{2,1,0:T(1,128)}), f32[32,1,4096]{2,1,0:T(1,128)S(1)}, u32[]{:S(2)}, u32[]{:S(2)}) async-start(f32[32,1,4096]{2,1,0:T(1,128)} %reshape.92), calls=%async_computation.3 | async-start | bytes 1048576 | tf_op jit(solution)/shard_map/all_to_all | solution.py:168
  415.4 177.4 %all-reduce.3.cloned.1.call-start = ((), (), s32[]{:S(2)}) async-start(), calls=%async_computation.4 | async-start | bytes 2097152 | tf_op jit(solution)/shard_map/psum | solution.py:205
  536.9 4.9 collective-permute-start.14
  545.0 50.1 %collective-permute-start.15 = (f32[16,32,3,128]{3,1,2,0:T(8,128)}, f32[16,32,3,128]{3,1,2,0:T(8,128)}, u32[]{:S(2)}, u32[]{:S(2)}) collective-permute-start(f32[16,32,3,128]{3,1,2,0:T(8,128)} %slice.127), channel_id=1, source_target_pairs={{0,1},{1,2},{2,3},{3,4},{4,5},{5,6},{6,7},{7,8},{8,9},{9,10},{10,1... | collective-permute-start | bytes 2359304 | tf_op jit(solution)/shard_map/ppermute | solution.py:24
  (9 other events, 26.0 us)
Sparse Core Ops, SparseCore 0:
  440.9 151.8 all-reduce.2
where the time goes:
time: 616 us; the launch traced here: 609 us
  waiting for transfers between devices  159 us (26%)
  blocking collectives  151 us (25%)
  local copies, waits for them, and re-layouts  122 us (20%)
  matrix products  119 us (19%)
  starting transfers between devices  29.7 us (5%)
  between operations  15.3 us (2%)
  other arithmetic  13.7 us (2%)
    ppermute x16, waiting for transfers between devices, from_behind(): lax.ppermute(value, axis, [(i, (i + by) % devices) for i in range(devices)])  106 us
    psum x1, blocking collectives, local(): point_total, bias_total = lax.psum((point_local, bias_local), ('gx', 'gy'))  77.5 us
    psum x1, waiting for transfers between devices, local(): mode_total = lax.psum(mode_local, 'gy')  41.4 us
    unnamed x56, local copies, waits for them, and re-layouts  40.1 us
    all_gather x2, blocking collectives, wave_block(): gathered = lax.all_gather(level_three, 'gx', axis=1, tiled=True)  31.6 us
    all_to_all x1, blocking collectives, wave_block(): lax.all_to_all(from_lanes(delta_one, channels), 'gy', split_axis=2, conca...  22 us
    dot_general x24, matrix products, plane_y(): jnp.einsum('kr,axr->axk', matrix, signal, precision=lax.Precision.HIGHEST)  20.3 us
    all_to_all x1, blocking collectives, wave_block(): lax.all_to_all(level_one, 'gy', split_axis=3, concat_axis=2, tiled=True)  19.5 us
  transfers between devices with their start and end apart: 19, of which 17 were waited for; matrix products, arithmetic and copies ran while one was open for 11% of the time, Pallas kernels for 0%

commit v1 on v0

--- a/solution.py
+++ b/solution.py
@@ -124,7 +124,14 @@
         filter_table(LOW_PASS, extent_y // 2, extent_y + 6, False),
         jnp.concatenate([halved, margin], 2),
     )
-    level_one = to_lanes(lax.all_to_all(level_one, "gy", split_axis=3, concat_axis=2, tiled=True))
+    level_one = to_lanes(
+        jnp.concatenate(
+            lax.all_to_all(
+                jnp.stack(jnp.split(level_one, lax.axis_size("gy"), axis=3)), "gy", 0, 0
+            ),
+            axis=2,
+        )
+    )
     rows_one, cols_one = (level_one.shape[1], level_one.shape[2])
     margin = from_behind(level_one[:, :6], "gx", -1)
     level_two = plane_x(

time: 616 us -> 710 us (1.15)
  local copies, waits for them, and re-layouts: 122 us -> 213 us
    unnamed x56 -> x108, local copies, waits for them, and re-layouts: 40.1 us -> 110 us
    another operation x0 -> x4, local copies, waits for them, and re-layouts: none -> 40.6 us  [wave_block(): jnp.stack(jnp.split(level_one, lax.axis_size('gy'), axis=3))]
    all_to_all x3 -> x1, local copies, waits for them, and re-layouts: 10.1 us -> 0.51 us  [wave_block(): lax.all_to_all(jnp.stack(jnp.split(level_one, lax.axis_size('gy'), axis=3...]
    transpose x2 -> x0, local copies, waits for them, and re-layouts: 8.83 us -> none  [along_y(): jnp.einsum('kr,axrs->axks', matrix, signal, precision=lax.Precision.HIGHEST)]
  transfers between devices with their start and end apart: 19 -> 19, of which waited for: 17 -> 17; matrix products, arithmetic and copies ran while one was open for 11% -> 9% of each run, Pallas kernels for 0% -> 0%
where the time goes in v1:
time: 710 us; the launch traced here: 706 us
  local copies, waits for them, and re-layouts  213 us (30%)
  waiting for transfers between devices  159 us (22%)
  blocking collectives  150 us (21%)
  matrix products  123 us (17%)
  starting transfers between devices  30.2 us (4%)
  between operations  15.3 us (2%)
  other arithmetic  13.5 us (2%)
    unnamed x108, local copies, waits for them, and re-layouts  110 us
    ppermute x16, waiting for transfers between devices, from_behind(): lax.ppermute(value, axis, [(i, (i + by) % devices) for i in range(devices)])  107 us
    psum x1, blocking collectives, local(): point_total, bias_total = lax.psum((point_local, bias_local), ('gx', 'gy'))  77.5 us
    psum x1, waiting for transfers between devices, local(): mode_total = lax.psum(mode_local, 'gy')  41.3 us
    another operation x4, local copies, waits for them, and re-layouts, wave_block(): jnp.stack(jnp.split(level_one, lax.axis_size('gy'), axis=3))  40.6 us
    all_gather x2, blocking collectives, wave_block(): gathered = lax.all_gather(level_three, 'gx', axis=1, tiled=True)  31.7 us
    all_to_all x1, blocking collectives, wave_block(): lax.all_to_all(from_lanes(delta_one, channels), 'gy', split_axis=2, conca...  22.1 us
    dot_general x24, matrix products, plane_y(): jnp.einsum('kr,axr->axk', matrix, signal, precision=lax.Precision.HIGHEST)  21 us
  transfers between devices with their start and end apart: 19, of which 17 were waited for; matrix products, arithmetic and copies ran while one was open for 9% of the time, Pallas kernels for 0%

profile of v1, /device:TPU:8, one launch (start us, length us, event | category | flops | bytes accessed | tf_op | source)
XLA Modules:
  0.0 705.6 jit_solution(13920406214901578323)
XLA Ops:
  9.3 6.7 collective-permute-done
  17.9 8.3 %collective-permute-start.1 = (f32[16,16,6,128]{3,1,2,0:T(8,128)S(1)}, f32[16,16,6,128]{3,1,2,0:T(8,128)S(1)}, u32[]{:S(2)}, u32[]{:S(2)}) collective-permute-start(f32[16,16,6,128]{3,1,2,0:T(8,128)S(1)} %slice.105), channel_id=1, source_target_pairs={{0,31},{1,0},{2,1},{3,2},{4,3},{5,4},{6,5},{7,6},{8,7},{9,8},{10,9... | collective-permute-start | bytes 2359304 | tf_op jit(solution)/shard_map/ppermute | solution.py:24
  26.2 17.1 %collective-permute-done.1 = f32[16,16,6,128]{3,1,2,0:T(8,128)S(1)} collective-permute-done((f32[16,16,6,128]{3,1,2,0:T(8,128)S(1)}, f32[16,16,6,128]{3,1,2,0:T(8,128)S(1)}, u32[]{:S(2)}, u32[]{:S(2)}) %collective-permute-start.1) | collective-permute-done | bytes 786464 | tf_op jit(solution)/shard_map/ppermute | solution.py:24
  81.7 19.2 %copy.267 = f32[32,16,16,4,4]{2,1,4,3,0:T(8,128)} copy(f32[32,16,16,4,4]{4,3,2,1,0:T(4,128)} %fusion.94) | data formatting | bytes 1048576 | tf_op jit(solution)/shard_map/stack | solution.py:130
  105.1 7.5 %all-to-all-start = ((f32[32,1,4096]{2,1,0:T(1,128)}), f32[32,1,4096]{2,1,0:T(1,128)S(1)}, u32[]{:S(2)}, u32[]{:S(2)}) async-start(f32[32,1,4096]{2,1,0:T(1,128)} %reshape.102), calls=%async_computation | async-start | bytes 1048576 | tf_op jit(solution)/shard_map/all_to_all | solution.py:129
  112.6 6.2 copy.356
  118.8 11.5 %all-to-all-done = f32[32,1,4096]{2,1,0:T(1,128)S(1)} async-done(((f32[32,1,4096]{2,1,0:T(1,128)}), f32[32,1,4096]{2,1,0:T(1,128)S(1)}, u32[]{:S(2)}, u32[]{:S(2)}) %all-to-all-start) | async-done | bytes 524320 | tf_op jit(solution)/shard_map/all_to_all | solution.py:129
  151.0 14.5 %all_gather.6 = f32[64,32,32]{0,2,1:T(8,128)S(1)} all-gather(f32[64,4,32]{0,2,1:T(8,128)S(1)} %fusion.187), channel_id=1, replica_groups=mesh['gx'=8,'gy'=32] {'gx'}, dimensions={1}, use_global_device_ids=true | all-gather | bytes 294912 | tf_op jit(solution)/shard_map/all_gather | solution.py:149
  171.9 14.6 %bitcast_subtract_fusion.1 = f32[4,16,4,16,16]{1,2,4,3,0:T(4,128)S(1)} fusion(f32[4,16,16,16,16]{2,1,4,3,0:T(8,128)} %bitcast.516, f32[1,16,4,16,16]{1,2,4,3,0:T(4,128)S(1)} %copy.283, f32[1,16,4,16,16]{1,2,4,3,0:T(4,128)S(1)} %copy.282, f32[1,16,4,16,16]{1,2,4,3,0:T(4,128)S(1)} %copy.281, f32[1,16,4,16,16]{1,2,4,3,0:T(4,128)S(1)} %copy.280), kind=kOutput, calls=%fused_computation.23 | convolution fusion | flops 13041664 | bytes 1572864 | tf_op jit(solution)/shard_map/bizxy,bioxy->bozxy/dot_general | solution.py:158
  197.0 4.8 collective-permute-done.4
  212.8 4.9 bitcast_bitcast_fusion.1
  221.1 22.1 %all_to_all.46 = f32[32,1,4096]{2,1,0:T(1,128)S(1)} all-to-all(f32[32,1,4096]{2,1,0:T(1,128)S(1)} %reshape.104), channel_id=1, replica_groups=mesh['gx'=8,'gy'=32] {'gy'}, dimensions={0} | all-to-all | bytes 1048576 | tf_op jit(solution)/shard_map/all_to_all | solution.py:175
  247.9 4.8 copy.298
  266.2 15.1 %collective-permute-done.7 = f32[16,32,3,128]{3,1,2,0:T(8,128)S(1)} collective-permute-done((f32[16,32,3,128]{3,1,2,0:T(8,128)S(1)}, f32[16,32,3,128]{3,1,2,0:T(8,128)S(1)}, u32[]{:S(2)}, u32[]{:S(2)}) %collective-permute-start.7) | collective-permute-done | bytes 786464 | tf_op jit(solution)/shard_map/ppermute | solution.py:24
  281.4 8.0 %fusion.1197 = (f32[16]{0:T(128)}, f32[16,32,8,128]{3,2,1,0:T(8,128)S(1)}, f32[16,32,8,128]{3,2,1,0:T(8,128)}) fusion(f32[16,32,8,128]{3,2,1,0:T(8,128)} %param.6, f32[16]{0:T(128)S(1)} %copy-done.16, f32[16,32,8,128]{3,0,2,1:T(8,128)S(1)} %fusion.27, f32[16,32,8,128]{3,2,1,0:T(8,128)} %param.5, s32[7]{0:T(128)S(1)} %iota_multiply_fusion.2, ...), kind=kOutput, calls=%fused_computation.1326 | convolution fusion | flops 56100200 | bytes 12320924 | tf_op jit(solution)/shard_map/kr,axrs->axks/dot_general | solution.py:54
  289.5 5.3 collective-permute-done.8
  297.5 19.6 %collective-permute-done.9 = f32[16,16,6,128]{3,1,2,0:T(8,128)S(1)} collective-permute-done((f32[16,16,6,128]{3,1,2,0:T(8,128)S(1)}, f32[16,16,6,128]{3,1,2,0:T(8,128)S(1)}, u32[]{:S(2)}, u32[]{:S(2)}) %collective-permute-start.9) | collective-permute-done | bytes 786464 | tf_op jit(solution)/shard_map/ppermute | solution.py:24
  355.6 19.2 %copy.307 = f32[32,16,16,4,4]{2,1,4,3,0:T(8,128)} copy(f32[32,16,16,4,4]{4,3,2,1,0:T(4,128)} %fusion.62) | data formatting | bytes 1048576 | tf_op jit(solution)/shard_map/stack | solution.py:130
  378.3 19.3 %all_to_all.47 = f32[32,1,4096]{2,1,0:T(1,128)S(1)} all-to-all(f32[32,1,4096]{2,1,0:T(1,128)S(1)} %reshape.106), channel_id=1, replica_groups=mesh['gx'=8,'gy'=32] {'gy'}, dimensions={0} | all-to-all | bytes 1048576 | tf_op jit(solution)/shard_map/all_to_all | solution.py:129
  412.9 5.2 collective-permute-done.11
  419.1 17.2 %all_gather.7 = f32[64,32,32]{0,2,1:T(8,128)S(1)} all-gather(f32[64,4,32]{0,2,1:T(8,128)S(1)} %fusion.183), channel_id=1, replica_groups=mesh['gx'=8,'gy'=32] {'gx'}, dimensions={1}, use_global_device_ids=true | all-gather | bytes 294912 | tf_op jit(solution)/shard_map/all_gather | solution.py:149
  444.2 18.0 %bitcast_subtract_fusion = f32[4,16,4,16,16]{1,2,4,3,0:T(4,128)S(1)} fusion(f32[4,16,16,16,16]{2,1,4,3,0:T(8,128)} %bitcast.517, f32[1,16,4,16,16]{1,2,4,3,0:T(4,128)} %copy.323, f32[1,16,4,16,16]{1,2,4,3,0:T(4,128)} %copy.322, f32[1,16,4,16,16]{1,2,4,3,0:T(4,128)} %copy.321, f32[1,16,4,16,16]{1,2,4,3,0:T(4,128)S(1)} %copy.320), kind=kOutput, calls=%fused_computation.19 | convolution fusion | flops 13041664 | bytes 1572864 | tf_op jit(solution)/shard_map/bozxy,bioxy->bizxy/dot_general | solution.py:154
  478.5 4.8 collective-permute-done.12
  496.2 4.7 bitcast_bitcast_fusion
  505.1 5.7 all-to-all-start.3
  510.9 17.6 %fusion.150 = f32[4,16,16,16,16]{4,3,2,1,0:T(8,128)} fusion(f32[1,16,4,16,16]{1,2,4,3,0:T(4,128)} %copy.323, f32[1,16,4,16,16]{1,2,4,3,0:T(4,128)} %copy.322, f32[1,16,4,16,16]{1,2,4,3,0:T(4,128)} %copy.321, f32[1,16,4,16,16]{1,2,4,3,0:T(4,128)} %copy-done.8, f32[1,16,4,16,16]{1,2,4,3,0:T(4,128)} %copy-done.7, f32[1,16,4,16,16]{1,2,4,3,0:T(4,128)} %copy-done.5, ...), kind=kOutput, calls=%fused_computation.234 | convolution fusion | flops 12976128 | bytes 1572864 | tf_op jit(solution)/shard_map/bizxy,bozxy->bioxy/dot_general | solution.py:208
  528.4 7.6 %copy.344 = f32[4,16,16,256]{3,2,1,0:T(8,128)} copy(f32[4,16,16,256]{1,2,3,0:T(8,128)} %bitcast.518) | data formatting | bytes 2097152 | tf_op jit(solution)/shard_map/reshape | solution.py:211
  536.0 6.3 fusion.45
  542.3 77.5 %all-reduce = (f32[16,16]{0,1:T(8,128)S(1)}, f32[16]{0:T(128)S(1)}) all-reduce(f32[16,16]{0,1:T(8,128)S(1)} %fusion.45, f32[16]{0:T(128)S(1)} %copy-done.15), channel_id=1, replica_groups=mesh['gx'=8,'gy'=32] {'gx','gy'}, use_global_device_ids=true, to_apply=%region_1.2 | all-reduce | flops 272 | bytes 2176 | tf_op jit(solution)/shard_map/psum | solution.py:217
  624.5 4.8 copy.338
  646.6 41.3 %all-reduce.3.cloned.1.call-done = f32[4,16,16,256]{3,2,1,0:T(8,128)} async-done(((f32[4,16,16,256]{3,2,1,0:T(8,128)}), f32[4,16,16,256]{3,2,1,0:T(8,128)}) %all-reduce.3.cloned.1.call-update) | async-done | bytes 1048592 | tf_op jit(solution)/shard_map/psum | solution.py:212
  691.6 6.9 bitcast_add_fusion
  (253 shorter events, 244.5 us)
Async XLA Ops:
  7.2 256.2 %copy-start = (f32[16,16]{1,0:T(8,128)S(1)}, f32[16,16]{1,0:T(8,128)}, u32[]{:S(2)}) copy-start(f32[16,16]{1,0:T(8,128)} %param.8) | copy-start | bytes 3076
  9.2 6.7 collective-permute-start
  17.9 25.4 %collective-permute-start.1 = (f32[16,16,6,128]{3,1,2,0:T(8,128)S(1)}, f32[16,16,6,128]{3,1,2,0:T(8,128)S(1)}, u32[]{:S(2)}, u32[]{:S(2)}) collective-permute-start(f32[16,16,6,128]{3,1,2,0:T(8,128)S(1)} %slice.105), channel_id=1, source_target_pairs={{0,31},{1,0},{2,1},{3,2},{4,3},{5,4},{6,5},{7,6},{8,7},{9,8},{10,9... | collective-permute-start | bytes 2359304 | tf_op jit(solution)/shard_map/ppermute | solution.py:24
  74.9 37.7 %copy-start.3 = (f32[4,16,16,256]{3,2,1,0:T(8,128)S(1)}, f32[4,16,16,256]{3,2,1,0:T(8,128)}, u32[]{:S(2)}) copy-start(f32[4,16,16,256]{3,2,1,0:T(8,128)} %param.7) | copy-start | bytes 3145732
  105.1 25.1 %all-to-all-start = ((f32[32,1,4096]{2,1,0:T(1,128)}), f32[32,1,4096]{2,1,0:T(1,128)S(1)}, u32[]{:S(2)}, u32[]{:S(2)}) async-start(f32[32,1,4096]{2,1,0:T(1,128)} %reshape.102), calls=%async_computation | async-start | bytes 1048576 | tf_op jit(solution)/shard_map/all_to_all | solution.py:129
  139.2 3.9 collective-permute-start.2
  144.2 5.8 collective-permute-start.3
  146.1 272.5 %copy-start.13 = (s32[32]{0:T(128)}, s32[32]{0:T(128)S(1)}, u32[]{:S(2)}) copy-start(s32[32]{0:T(128)S(1)} %iota_multiply_fusion.3) | copy-start | bytes 388
  169.1 2.0 copy-start.4
  196.8 5.0 collective-permute-start.4
  197.0 84.5 %copy-start.9 = (s32[7]{0:T(128)}, s32[7]{0:T(128)S(1)}, u32[]{:S(2)}) copy-start(s32[7]{0:T(128)S(1)} %iota_multiply_fusion.2) | copy-start | bytes 88
  202.7 4.1 collective-permute-start.5
  202.7 49.9 %copy-start.14 = (s32[11]{0:T(128)}, s32[11]{0:T(128)S(1)}, u32[]{:S(2)}) copy-start(s32[11]{0:T(128)S(1)} %iota_multiply_fusion.1) | copy-start | bytes 136
  212.8 50.6 %copy-start.1 = (f32[16,32,8,128]{3,2,1,0:T(8,128)S(1)}, f32[16,32,8,128]{3,2,1,0:T(8,128)}, u32[]{:S(2)}) copy-start(f32[16,32,8,128]{3,2,1,0:T(8,128)} %param.5) | copy-start | bytes 6291460
  221.1 60.3 %copy-start.16 = (f32[16]{0:T(128)S(1)}, f32[16]{0:T(128)}, u32[]{:S(2)}) copy-start(f32[16]{0:T(128)} %param.9) | copy-start | bytes 196
  255.5 4.4 collective-permute-start.6
  255.5 41.4 %copy-start.11 = (s32[19]{0:T(128)}, s32[19]{0:T(128)S(1)}, u32[]{:S(2)}) copy-start(s32[19]{0:T(128)S(1)} %iota_multiply_fusion) | copy-start | bytes 232
  261.1 20.2 %collective-permute-start.7 = (f32[16,32,3,128]{3,1,2,0:T(8,128)S(1)}, f32[16,32,3,128]{3,1,2,0:T(8,128)S(1)}, u32[]{:S(2)}, u32[]{:S(2)}) collective-permute-start(f32[16,32,3,128]{3,1,2,0:T(8,128)S(1)} %slice.115), channel_id=1, source_target_pairs={{0,1},{1,2},{2,3},{3,4},{4,5},{5,6},{6,7},{7,8},{8,9},{9,10},{10,1... | collective-permute-start | bytes 2359304 | tf_op jit(solution)/shard_map/ppermute | solution.py:24
  289.4 5.3 collective-permute-start.8
  297.0 20.1 %collective-permute-start.9 = (f32[16,16,6,128]{3,1,2,0:T(8,128)S(1)}, f32[16,16,6,128]{3,1,2,0:T(8,128)S(1)}, u32[]{:S(2)}, u32[]{:S(2)}) collective-permute-start(f32[16,16,6,128]{3,1,2,0:T(8,128)S(1)} %slice.117), channel_id=1, source_target_pairs={{0,31},{1,0},{2,1},{3,2},{4,3},{5,4},{6,5},{7,6},{8,7},{9,8},{10,9... | collective-permute-start | bytes 2359304 | tf_op jit(solution)/shard_map/ppermute | solution.py:24
  406.0 3.9 collective-permute-start.10
  411.0 7.1 %collective-permute-start.11 = (f32[64,6,64]{2,1,0:T(8,128)S(1)}, f32[64,6,64]{2,1,0:T(8,128)S(1)}, u32[]{:S(2)}, u32[]{:S(2)}) collective-permute-start(f32[64,6,64]{2,1,0:T(8,128)S(1)} %bitcast.542), channel_id=1, source_target_pairs={{0,224},{32,0},{64,32},{96,64},{128,96},{160,128},{192,160},{224,1... | collective-permute-start | bytes 294920 | tf_op jit(solution)/shard_map/ppermute | solution.py:24
  439.9 4.3 copy-start.8
  478.3 5.0 collective-permute-start.12
  485.5 4.1 collective-permute-start.13
  500.9 41.4 %copy-start.15 = (f32[16]{0:T(128)S(1)}, f32[16]{0:T(128)}, u32[]{:S(2)}) copy-start(f32[16]{0:T(128)} %get-tuple-element.27) | copy-start | bytes 196
  505.1 114.7 %all-to-all-start.3 = ((f32[32,1,4096]{2,1,0:T(1,128)}), f32[32,1,4096]{2,1,0:T(1,128)S(1)}, u32[]{:S(2)}, u32[]{:S(2)}) async-start(f32[32,1,4096]{2,1,0:T(1,128)} %reshape.108), calls=%async_computation.3 | async-start | bytes 1048576 | tf_op jit(solution)/shard_map/all_to_all | solution.py:175
  510.8 177.1 %all-reduce.3.cloned.1.call-start = ((), (), s32[]{:S(2)}) async-start(), calls=%async_computation.4 | async-start | bytes 2097152 | tf_op jit(solution)/shard_map/psum | solution.py:212
  528.4 108.6 %copy-start.12 = (s32[19]{0:T(128)S(1)}, s32[19]{0:T(128)}, u32[]{:S(2)}) copy-start(s32[19]{0:T(128)} %copy-done.11) | copy-start | bytes 232
  542.3 149.3 %copy-start.10 = (s32[7]{0:T(128)S(1)}, s32[7]{0:T(128)}, u32[]{:S(2)}) copy-start(s32[7]{0:T(128)} %copy-done.9) | copy-start | bytes 88
  632.1 4.9 collective-permute-start.14
  640.1 50.1 %collective-permute-start.15 = (f32[16,32,3,128]{3,1,2,0:T(8,128)}, f32[16,32,3,128]{3,1,2,0:T(8,128)}, u32[]{:S(2)}, u32[]{:S(2)}) collective-permute-start(f32[16,32,3,128]{3,1,2,0:T(8,128)} %slice.127), channel_id=1, source_target_pairs={{0,1},{1,2},{2,3},{3,4},{4,5},{5,6},{6,7},{7,8},{8,9},{9,10},{10,1... | collective-permute-start | bytes 2359304 | tf_op jit(solution)/shard_map/ppermute | solution.py:24
  (4 other events, 3.8 us)
Sparse Core Ops, SparseCore 0:
  536.1 151.7 all-reduce.2
